TPU v7x, 256 devices: a whole 4x4x8 slice. The times are simulated.
256 devices in a mesh: dp: 32 (over y, x, core), tensor: 8 (over z).
Axes of the slice: x: 4, y: 4, z: 8, core: 2. Of those that a mesh axis runs over, the one named last changes fastest.
Arguments:
- patches: bfloat16 [16384, 1280], P('dp'), may hold values from -6 to 6
- window_ids: int32 [32, 512], P('dp'), may hold values from 0 to 15, never falling along the last dimension, each value on 1 to 64 neighbouring positions
- vit_gain: float32 [1280], replicated, may hold values from 0.5 to 2
- qkv_weight: bfloat16 [3, 1280, 1280], P(None, None, 'tensor'), may hold values from -0.15625 to 0.15625
- out_weight: bfloat16 [1280, 1280], P('tensor'), may hold values from -0.15625 to 0.15625
- merge_gain: float32 [1280], replicated, may hold values from 0.5 to 2
- merger_weight: bfloat16 [5120, 3584], P(None, 'tensor'), may hold values from -0.078125 to 0.078125
- audio: bfloat16 [12288, 3584], P('dp', 'tensor'), may hold values from -6 to 6
- span_lengths: int32 [32, 32], replicated, may hold values from 8 to 32, as said below
- span_time: int32 [32, 32], replicated, may hold values from 0 to 31, each once within a row
- llm_gain: float32 [3584], replicated, may hold values from 0.5 to 2
- gate_weight: bfloat16 [3584, 9472], P('dp', 'tensor'), may hold values from -0.09375 to 0.09375
- up_weight: bfloat16 [3584, 9472], P('dp', 'tensor'), may hold values from -0.09375 to 0.09375
- down_weight: bfloat16 [9472, 3584], P('tensor', 'dp'), may hold values from -0.0625 to 0.0625
Outputs:
- mixed: bfloat16 [16384, 3584], P(('dp', 'tensor'))
Inputs may be any that keep to these rules, and one draw needn't show every extreme that they name: `span_lengths`: every row and every column sums to 512; every row and every column holds the value 32 at least once. `span_time`: each row is a permutation of the owners' numbers. `window_ids`: window numbers never fall along a row; a window holds at most 64 patches.
All inputs are finite; a program needn't handle non-finite values.
Results may differ from a plain program's by a relative error of at most 0.017.
Values may be sent and summed in bfloat16 or wider, within the bound.
No kernel may reach another device: no remote copies, remote signals or barrier semaphores. Data moves between devices by JAX's collectives and lax.ppermute only.
A program may use at most 128 MiB of HBM per device.

v0:
```python
import math
import jax
import jax.numpy as jnp
from jax import lax
from jax.sharding import PartitionSpec as P

D_VIT = 1280
HEAD_VIT = 80
EPSILON = 1e-06


def in_blocks(x, dim, devices):
    before, after = (x.shape[:dim], x.shape[dim + 1 :])
    return jnp.moveaxis(x.reshape(*before, devices, -1, *after), dim, 0)


def sent_and_summed(x, axis, dim):
    parts = in_blocks(x, dim, lax.axis_size(axis))
    arrived = lax.all_to_all(parts, axis, split_axis=0, concat_axis=0, tiled=True)
    return arrived.astype(jnp.float32).sum(axis=0)


def from_everyone(x, axis):
    devices = lax.axis_size(axis)
    return lax.all_to_all(jnp.broadcast_to(x[None], (devices, *x.shape)), axis, 0, 0, tiled=True)


def in_order(parts, dim):
    parts = jnp.moveaxis(parts, 0, dim)
    dims = parts.shape
    return parts.reshape(*dims[:dim], dims[dim] * dims[dim + 1], *dims[dim + 2 :])


def gather_directly(x, axis, dim):
    parts = from_everyone(x, axis)
    return in_order(parts, dim)


def gather_turned(arrays, axis, dims):
    turned = [jnp.moveaxis(a, dim, 0) for a, dim in zip(arrays, dims)]
    widths = [t[0].size for t in turned]
    both = jnp.concatenate([t.reshape(-1, w) for t, w in zip(turned, widths)], axis=1)
    whole = lax.all_gather(both, axis, axis=0, tiled=True)
    parts = jnp.split(whole, [sum(widths[:k]) for k in range(1, len(widths))], axis=1)
    return tuple(
        (
            jnp.moveaxis(b.reshape(-1, *t.shape[1:]), 0, dim)
            for b, t, dim in zip(parts, turned, dims)
        )
    )


def rms_scale(values, gain):
    wide = values.astype(jnp.float32)
    meansq = jnp.mean(wide * wide, axis=-1, keepdims=True)
    return wide * lax.rsqrt(meansq + EPSILON) * gain


def body(
    patches,
    window_ids,
    vit_gain,
    qkv_weight,
    out_weight,
    merge_gain,
    merger_weight,
    audio,
    span_lengths,
    span_time,
    llm_gain,
    gate_weight,
    up_weight,
    down_weight,
):
    patch_count = patches.shape[0]
    heads_here = qkv_weight.shape[2] // HEAD_VIT
    normed = rms_scale(patches, vit_gain).astype(jnp.bfloat16)
    query = jnp.dot(normed, qkv_weight[0], preferred_element_type=jnp.float32).astype(jnp.bfloat16)
    keys = jnp.dot(normed, qkv_weight[1], preferred_element_type=jnp.float32).astype(jnp.bfloat16)
    values = jnp.dot(normed, qkv_weight[2], preferred_element_type=jnp.float32).astype(jnp.bfloat16)
    query = query.reshape(patch_count, heads_here, HEAD_VIT)
    keys = keys.reshape(patch_count, heads_here, HEAD_VIT)
    values = values.reshape(patch_count, heads_here, HEAD_VIT)
    scores = jnp.einsum(
        "phe,qhe->hpq", query, keys, preferred_element_type=jnp.float32
    ) / math.sqrt(HEAD_VIT)
    windows = window_ids[0]
    same = windows[:, None] == windows[None, :]
    scores = jnp.where(same[None], scores, -1e30)
    probs = jax.nn.softmax(scores, axis=-1).astype(jnp.bfloat16)
    context = jnp.einsum("hpq,qhe->phe", probs, values, preferred_element_type=jnp.float32).astype(
        jnp.bfloat16
    )
    context = context.reshape(patch_count, heads_here * HEAD_VIT)
    partial_value = jnp.dot(context, out_weight, preferred_element_type=jnp.float32)
    share = sent_and_summed(partial_value.astype(jnp.bfloat16), "tensor", 0)
    share_rows = share.shape[0]
    own_frames = lax.dynamic_slice_in_dim(
        patches, lax.axis_index("tensor") * share_rows, share_rows, 0
    )
    own_encoded = (own_frames.astype(jnp.float32) + share).astype(jnp.bfloat16)
    encoded = gather_directly(own_encoded, "tensor", 0)
    merged = (
        rms_scale(encoded, merge_gain).astype(jnp.bfloat16).reshape(patch_count // 4, 4 * D_VIT)
    )
    video = jnp.dot(merged, merger_weight, preferred_element_type=jnp.float32).astype(jnp.bfloat16)
    source = jnp.concatenate([video, audio], axis=0)
    seq_count = source.shape[0]
    owner_count = lax.axis_size("dp")
    owner = lax.axis_index("dp")
    capacity = 2 * seq_count // owner_count
    sent_lengths = span_lengths[owner]
    starts = jnp.cumsum(sent_lengths) - sent_lengths
    slot_index = jnp.arange(capacity, dtype=jnp.int32)
    occupied = slot_index[None, :] < sent_lengths[:, None]
    source_index = jnp.where(occupied, starts[:, None] + slot_index[None, :], 0).reshape(-1)
    outgoing = jnp.take(source, source_index, axis=0)
    outgoing = jnp.where(occupied.reshape(-1)[:, None], outgoing, jnp.zeros((), outgoing.dtype))
    incoming = lax.all_to_all(outgoing, "dp", split_axis=0, concat_axis=0, tiled=True)
    taken_lengths = span_lengths[:, owner]
    arrival = span_time[owner]
    earlier = arrival[:, None] < arrival[None, :]
    offsets = jnp.sum(jnp.where(earlier, taken_lengths[:, None], 0), axis=0)
    position = jnp.arange(seq_count, dtype=jnp.int32)
    inside = (position[None, :] >= offsets[:, None]) & (
        position[None, :] < offsets[:, None] + taken_lengths[:, None]
    )
    sender = jnp.arange(owner_count, dtype=jnp.int32)[:, None]
    slot_row = sender * capacity + position[None, :] - offsets[:, None]
    picked = jnp.sum(jnp.where(inside, slot_row, 0), axis=0)
    sequence = jnp.take(incoming, picked, axis=0)
    features = lax.all_gather(sequence, "tensor", axis=1, tiled=True)
    normed_seq = rms_scale(features, llm_gain).astype(jnp.bfloat16)
    gate_full, up_full, down_full = gather_turned(
        (gate_weight, up_weight, down_weight), "dp", (0, 0, 1)
    )
    gate = jnp.dot(normed_seq, gate_full, preferred_element_type=jnp.float32)
    upward = jnp.dot(normed_seq, up_full, preferred_element_type=jnp.float32)
    hidden = (jax.nn.silu(gate) * upward).astype(jnp.bfloat16)
    terms = jnp.dot(hidden, down_full, preferred_element_type=jnp.float32)
    summed = lax.psum_scatter(
        terms.astype(jnp.bfloat16), "tensor", scatter_dimension=0, tiled=True
    ).astype(jnp.float32)
    own_count = summed.shape[0]
    own_rows = lax.dynamic_slice_in_dim(
        features, lax.axis_index("tensor") * own_count, own_count, 0
    )
    return (own_rows.astype(jnp.float32) + summed).astype(jnp.bfloat16)


def solution(mesh):
    return jax.shard_map(
        body,
        mesh=mesh,
        in_specs=(
            P("dp", None),
            P("dp", None),
            P(),
            P(None, None, "tensor"),
            P("tensor", None),
            P(),
            P(None, "tensor"),
            P("dp", "tensor"),
            P(),
            P(),
            P(),
            P("dp", "tensor"),
            P("dp", "tensor"),
            P("tensor", "dp"),
        ),
        out_specs=P(("dp", "tensor"), None),
        check_vma=False,
    )
```

profile of v0, /device:TPU:1, one launch (start us, length us, event | category | flops | bytes accessed | tf_op | source)
XLA Modules:
  0.0 377.8 jit_solution(1047735685525039576)
XLA Ops:
  6.5 1.8 fusion.19
  8.4 2.1 convolution_convert_fusion.3
  14.3 1.6 convolution_convert_fusion
  15.9 9.0 %all-to-all-start = ((bf16[8,64,1280]{2,1,0:T(8,128)(2,1)}), bf16[8,64,1280]{2,1,0:T(8,128)(2,1)S(1)}, u32[]{:S(2)}, u32[]{:S(2)}) async-start(bf16[8,64,1280]{2,1,0:T(8,128)(2,1)} %bitcast.15), calls=%async_computation | async-start | bytes 2621440 | tf_op jit(solution)/shard_map/all_to_all | solution.py:19
  24.9 34.9 %all-to-all-done = bf16[8,64,1280]{2,1,0:T(8,128)(2,1)S(1)} async-done(((bf16[8,64,1280]{2,1,0:T(8,128)(2,1)}), bf16[8,64,1280]{2,1,0:T(8,128)(2,1)S(1)}, u32[]{:S(2)}, u32[]{:S(2)}) %all-to-all-start) | async-done | bytes 1310752 | tf_op jit(solution)/shard_map/all_to_all | solution.py:19
  61.2 3.6 all-to-all-start.1
  66.6 32.9 %all-to-all-done.1 = bf16[8,64,1280]{2,1,0:T(8,128)(2,1)S(1)} async-done(((bf16[8,64,1280]{2,1,0:T(8,128)(2,1)}), bf16[8,64,1280]{2,1,0:T(8,128)(2,1)S(1)}, u32[]{:S(2)}, u32[]{:S(2)}) %all-to-all-start.1) | async-done | bytes 1310752 | tf_op jit(solution)/shard_map/all_to_all | solution.py:25
  100.4 2.0 copy.42
  102.3 1.9 reshape.242
  104.2 5.2 %fusion.25 = bf16[128,448]{0,1:T(8,128)(2,1)S(1)} fusion(bf16[5120,448]{0,1:T(8,128)(2,1)} %param.20, f32[128,5120]{1,0:T(8,128)} %reshape.242, f32[128,5120]{1,0:T(8,128)} %bitcast.49, f32[5120]{0:T(1024)S(1)} %mul.101), kind=kOutput, calls=%fused_computation.36 | convolution fusion | flops 589225984 | bytes 9965568 | tf_op jit(solution)/shard_map/dot_general | solution.py:106
  109.6 4.0 %gather_fusion = bf16[1024,448]{1,0:T(8,128)(2,1)S(1)} fusion(bf16[512,448]{1,0:T(8,128)(2,1)S(1)} %pad_maximum_fusion, s32[1024]{0:T(1024)S(1)} %broadcast_clamp_fusion), kind=kCustom, calls=%fused_computation | custom fusion | bytes 1839104 | tf_op jit(solution)/shard_map/jit(_take)/gather | solution.py:117
  113.6 1.3 select_select_fusion
  114.9 7.6 %all-to-all-start.2 = ((bf16[32,32,448]{2,1,0:T(8,128)(2,1)}), bf16[32,32,448]{2,1,0:T(8,128)(2,1)S(1)}, u32[]{:S(2)}, u32[]{:S(2)}) async-start(bf16[32,32,448]{2,1,0:T(8,128)(2,1)} %select_select_fusion), calls=%async_computation.2 | async-start | bytes 2097152 | tf_op jit(solution)/shard_map/all_to_all | solution.py:119
  122.6 17.0 %all-to-all-done.2 = bf16[32,32,448]{2,1,0:T(8,128)(2,1)S(1)} async-done(((bf16[32,32,448]{2,1,0:T(8,128)(2,1)}), bf16[32,32,448]{2,1,0:T(8,128)(2,1)S(1)}, u32[]{:S(2)}, u32[]{:S(2)}) %all-to-all-start.2) | async-done | bytes 917536 | tf_op jit(solution)/shard_map/all_to_all | solution.py:119
  139.6 2.0 gather_fusion.1
  142.8 1.4 concatenate.7
  144.4 40.7 %all-gather.3.cloned.1.call-done = bf16[512,3584]{0,1:T(8,128)(2,1)} async-done(((bf16[512,448]{0,1:T(8,128)(2,1)}), bf16[512,3584]{0,1:T(8,128)(2,1)}) %all-gather.3.cloned.1.call-update) | async-done | bytes 3670032 | tf_op jit(solution)/shard_map/all_gather | solution.py:132
  185.1 2.9 fusion.7
  188.0 97.1 %all-gather.5.cloned.1.call-done = bf16[3584,3552]{1,0:T(8,128)(2,1)} async-done(((bf16[112,3552]{1,0:T(8,128)(2,1)}), bf16[3584,3552]{1,0:T(8,128)(2,1)}) %all-gather.5.cloned.1.call-update) | async-done | bytes 25460752 | tf_op jit(solution)/shard_map/all_gather | solution.py:43
  285.1 9.8 %fusion.5 = f32[512,1184]{0,1:T(8,128)S(1)} fusion(bf16[3584,3552]{1,0:T(8,128)(2,1)} %all-gather.5.cloned.1.call-done, bf16[512,3584]{0,1:T(8,128)(2,1)} %all-gather.3.cloned.1.call-done, f32[3584]{0:T(1024)S(1)} %copy-done.11, f32[512]{0:T(512)S(1)} %add_rsqrt_fusion.1), kind=kOutput, calls=%fused_computation.7 | convolution fusion | flops 4352638976 | bytes 15286272 | tf_op jit(solution)/shard_map/dot_general | solution.py:137
  294.9 24.9 %fusion.10 = bf16[512,3584]{1,0:T(8,128)(2,1)} fusion(bf16[3584,3552]{1,0:T(8,128)(2,1)} %all-gather.5.cloned.1.call-done, f32[512,1184]{0,1:T(8,128)S(1)} %fusion.5, bf16[512,3584]{0,1:T(8,128)(2,1)} %all-gather.3.cloned.1.call-done, f32[3584]{0:T(1024)S(1)} %copy-done.11, f32[512]{0:T(512)S(1)} %add_rsqrt_fusion.1), kind=kOutput, calls=%fused_computation.14 | convolution fusion | flops 8703410176 | bytes 28131328 | tf_op jit(solution)/shard_map/dot_general | solution.py:140
  319.8 1.6 constant_dynamic-slice_fusion
  321.7 47.7 %reduce-scatter.2.cloned.1.call-done = bf16[64,3584]{1,0:T(8,128)(2,1)} async-done(((bf16[512,3584]{1,0:T(8,128)(2,1)}), bf16[64,3584]{1,0:T(8,128)(2,1)}) %reduce-scatter.2.cloned.1.call-update) | async-done | bytes 458768 | tf_op jit(solution)/shard_map/reduce_scatter | solution.py:141
  369.4 1.9 add_convert_fusion
  (74 shorter events, 9.8 us)
Async XLA Ops:
  6.5 7.7 %copy-start = (bf16[160,1280]{1,0:T(8,128)(2,1)S(1)}, bf16[160,1280]{1,0:T(8,128)(2,1)}, u32[]{:S(2)}) copy-start(bf16[160,1280]{1,0:T(8,128)(2,1)} %param.18) | copy-start | bytes 1228804
  6.5 3.9 %copy-start.2 = (bf16[512,1280]{1,0:T(8,128)(2,1)S(1)}, bf16[512,1280]{1,0:T(8,128)(2,1)}, u32[]{:S(2)}) copy-start(bf16[512,1280]{1,0:T(8,128)(2,1)} %param.14) | copy-start | bytes 3932164
  6.5 3.9 %copy-start.12 = (f32[1280]{0:T(1024)S(1)}, f32[1280]{0:T(1024)}, u32[]{:S(2)}) copy-start(f32[1280]{0:T(1024)} %param.16) | copy-start | bytes 15364
  6.5 3.9 %copy-start.10 = (bf16[3,1280,160]{1,2,0:T(8,128)(2,1)S(1)}, bf16[3,1280,160]{1,2,0:T(8,128)(2,1)}, u32[]{:S(2)}) copy-start(bf16[3,1280,160]{1,2,0:T(8,128)(2,1)} %param.17) | copy-start | bytes 3686404
  10.5 1.3 copy-start.8
  15.9 43.9 %all-to-all-start = ((bf16[8,64,1280]{2,1,0:T(8,128)(2,1)}), bf16[8,64,1280]{2,1,0:T(8,128)(2,1)S(1)}, u32[]{:S(2)}, u32[]{:S(2)}) async-start(bf16[8,64,1280]{2,1,0:T(8,128)(2,1)} %bitcast.15), calls=%async_computation | async-start | bytes 2621440 | tf_op jit(solution)/shard_map/all_to_all | solution.py:19
  60.0 4.8 %copy-start.9 = (f32[1280]{0:T(1024)S(1)}, f32[1280]{0:T(1024)}, u32[]{:S(2)}) copy-start(f32[1280]{0:T(1024)} %param.19) | copy-start | bytes 15364
  60.0 4.8 %copy-start.3 = (bf16[384,448]{0,1:T(8,128)(2,1)S(1)}, bf16[384,448]{0,1:T(8,128)(2,1)}, u32[]{:S(2)}) copy-start(bf16[384,448]{0,1:T(8,128)(2,1)} %param.21) | copy-start | bytes 1032196
  60.0 5.0 %copy-start.7 = (s32[32,32]{1,0:T(8,128)S(1)}, s32[32,32]{1,0:T(8,128)}, u32[]{:S(2)}) copy-start(s32[32,32]{1,0:T(8,128)} %param.22) | copy-start | bytes 12292
  61.2 38.3 %all-to-all-start.1 = ((bf16[8,64,1280]{2,1,0:T(8,128)(2,1)}), bf16[8,64,1280]{2,1,0:T(8,128)(2,1)S(1)}, u32[]{:S(2)}, u32[]{:S(2)}) async-start(bf16[8,64,1280]{2,1,0:T(8,128)(2,1)} %broadcast_in_dim.103), calls=%async_computation.1 | async-start | bytes 2621440 | tf_op jit(solution)/shard_map/all_to_all | solution.py:25
  114.9 24.8 %all-to-all-start.2 = ((bf16[32,32,448]{2,1,0:T(8,128)(2,1)}), bf16[32,32,448]{2,1,0:T(8,128)(2,1)S(1)}, u32[]{:S(2)}, u32[]{:S(2)}) async-start(bf16[32,32,448]{2,1,0:T(8,128)(2,1)} %select_select_fusion), calls=%async_computation.2 | async-start | bytes 2097152 | tf_op jit(solution)/shard_map/all_to_all | solution.py:119
  122.4 62.7 %all-gather.3.cloned.1.call-start = ((), (), s32[]{:S(2)}) async-start(), calls=%async_computation.4 | async-start | bytes 4128768 | tf_op jit(solution)/shard_map/all_gather | solution.py:132
  139.6 3.2 copy-start.4
  139.6 3.2 copy-start.5
  139.6 3.2 copy-start.6
  142.7 142.4 %all-gather.5.cloned.1.call-start = ((), (), s32[]{:S(2)}) async-start(), calls=%async_computation.5 | async-start | bytes 26492928 | tf_op jit(solution)/shard_map/all_gather | solution.py:43
  144.1 141.0 %copy-start.11 = (f32[3584]{0:T(1024)S(1)}, f32[3584]{0:T(1024)}, u32[]{:S(2)}) copy-start(f32[3584]{0:T(1024)} %param.24) | copy-start | bytes 43012
  144.2 225.2 %reduce-scatter.2.cloned.1.call-start = ((), (), s32[]{:S(2)}) async-start(), calls=%async_computation.6 | async-start | bytes 4128768 | tf_op jit(solution)/shard_map/reduce_scatter | solution.py:141
  319.8 51.5 %copy-start.1 = (bf16[160,1280]{1,0:T(8,128)(2,1)S(1)}, bf16[160,1280]{1,0:T(8,128)(2,1)}, u32[]{:S(2)}) copy-start(bf16[160,1280]{1,0:T(8,128)(2,1)} %param.18) | copy-start | bytes 1228804
Sparse Core Ops, SparseCore 0:
  142.8 42.2 all-gather.2
  187.7 97.3 all-gather.4
  319.9 49.4 reduce-scatter.1
where the time goes:
time: 378 us
  waiting for transfers between devices  270 us (71%)
  matrix products  47.1 us (12%)
  starting transfers between devices  20.5 us (5%)
  local copies, waits for them, and re-layouts  17 us (4%)
  between operations  13.5 us (4%)
  other arithmetic  9.35 us (2%)
    all_gather x1, waiting for transfers between devices, gather_turned(): whole = lax.all_gather(both, axis, axis=0, tiled=True)  97.1 us
    reduce_scatter x1, waiting for transfers between devices, body(): lax.psum_scatter(terms.astype(jnp.bfloat16), 'tensor', scatter_dimension=...  47.7 us
    all_gather x1, waiting for transfers between devices, body(): features = lax.all_gather(sequence, 'tensor', axis=1, tiled=True)  40.7 us
    all_to_all x1, waiting for transfers between devices, sent_and_summed(): lax.all_to_all(parts, axis, split_axis=0, concat_axis=0, tiled=True)  34.9 us
    all_to_all x1, waiting for transfers between devices, from_everyone(): lax.all_to_all(jnp.broadcast_to(x[None], (devices, *x.shape)), axis, 0, 0...  32.9 us
    dot_general x1, matrix products, body(): terms = jnp.dot(hidden, down_full, preferred_element_type=jnp.float32)  24.9 us
    all_to_all x1, waiting for transfers between devices, body(): lax.all_to_all(outgoing, 'dp', split_axis=0, concat_axis=0, tiled=True)  17 us
    dot_general x1, matrix products, body(): gate = jnp.dot(normed_seq, gate_full, preferred_element_type=jnp.float32)  9.77 us
  transfers between devices with their start and end apart: 6, of which 6 were waited for; matrix products, arithmetic and copies ran while one was open for 2% of the time, Pallas kernels for 0%

commit v1 on v0

--- a/solution.py
+++ b/solution.py
@@ -40,7 +40,9 @@
     turned = [jnp.moveaxis(a, dim, 0) for a, dim in zip(arrays, dims)]
     widths = [t[0].size for t in turned]
     both = jnp.concatenate([t.reshape(-1, w) for t, w in zip(turned, widths)], axis=1)
-    whole = lax.all_gather(both, axis, axis=0, tiled=True)
+    whole = jnp.concatenate(
+        lax.all_to_all(jnp.stack([both] * lax.axis_size(axis)), axis, 0, 0), axis=0
+    )
     parts = jnp.split(whole, [sum(widths[:k]) for k in range(1, len(widths))], axis=1)
     return tuple(
         (

time: 378 us -> 568 us (1.50)
  waiting for transfers between devices: 270 us -> 446 us
  local copies, waits for them, and re-layouts: 17 us -> 24.8 us
    all_to_all x0 -> x1, waiting for transfers between devices: none -> 257 us  [gather_turned(): lax.all_to_all(jnp.stack([both] * lax.axis_size(axis)), axis, 0, 0)]
    all_gather x1 -> x0, waiting for transfers between devices: 97.1 us -> none  [gather_turned(): whole = lax.all_gather(both, axis, axis=0, tiled=True)]
    reduce_scatter x1, waiting for transfers between devices: 47.7 us -> 57.7 us  [body(): lax.psum_scatter(terms.astype(jnp.bfloat16), 'tensor', scatter_dimension=...]
    another operation x2 -> x3, local copies, waits for them, and re-layouts: 0.1 us -> 8.68 us  [the longest x1 8.58 us: gather_turned(): jnp.stack([both] * lax.axis_size(axis))]
where the time goes in v1:
time: 568 us; the launch traced here: 567 us
  waiting for transfers between devices  446 us (79%)
  matrix products  47 us (8%)
  starting transfers between devices  25.8 us (5%)
  local copies, waits for them, and re-layouts  24.8 us (4%)
  between operations  13.8 us (2%)
  other arithmetic  9.36 us (2%)
    all_to_all x1, waiting for transfers between devices, gather_turned(): lax.all_to_all(jnp.stack([both] * lax.axis_size(axis)), axis, 0, 0)  257 us
    reduce_scatter x1, waiting for transfers between devices, body(): lax.psum_scatter(terms.astype(jnp.bfloat16), 'tensor', scatter_dimension=...  57.7 us
    all_gather x1, waiting for transfers between devices, body(): features = lax.all_gather(sequence, 'tensor', axis=1, tiled=True)  45.9 us
    all_to_all x1, waiting for transfers between devices, sent_and_summed(): lax.all_to_all(parts, axis, split_axis=0, concat_axis=0, tiled=True)  34.9 us
    all_to_all x1, waiting for transfers between devices, from_everyone(): lax.all_to_all(jnp.broadcast_to(x[None], (devices, *x.shape)), axis, 0, 0...  33.9 us
    dot_general x1, matrix products, body(): terms = jnp.dot(hidden, down_full, preferred_element_type=jnp.float32)  24.9 us
    all_to_all x1, waiting for transfers between devices, body(): lax.all_to_all(outgoing, 'dp', split_axis=0, concat_axis=0, tiled=True)  16.6 us
  transfers between devices with their start and end apart: 6, of which 6 were waited for; matrix products, arithmetic and copies ran while one was open for 2% of the time, Pallas kernels for 0%

profile of v1, /device:TPU:1, one launch (start us, length us, event | category | flops | bytes accessed | tf_op | source)
XLA Modules:
  0.0 567.2 jit_solution(12623454068268925336)
XLA Ops:
  6.5 1.8 fusion.19
  8.4 2.1 convolution_convert_fusion.4
  14.3 1.6 convolution_convert_fusion
  15.9 9.0 %all-to-all-start = ((bf16[8,64,1280]{2,1,0:T(8,128)(2,1)}), bf16[8,64,1280]{2,1,0:T(8,128)(2,1)S(1)}, u32[]{:S(2)}, u32[]{:S(2)}) async-start(bf16[8,64,1280]{2,1,0:T(8,128)(2,1)} %bitcast.15), calls=%async_computation | async-start | bytes 2621440 | tf_op jit(solution)/shard_map/all_to_all | solution.py:19
  24.9 34.9 %all-to-all-done = bf16[8,64,1280]{2,1,0:T(8,128)(2,1)S(1)} async-done(((bf16[8,64,1280]{2,1,0:T(8,128)(2,1)}), bf16[8,64,1280]{2,1,0:T(8,128)(2,1)S(1)}, u32[]{:S(2)}, u32[]{:S(2)}) %all-to-all-start) | async-done | bytes 1310752 | tf_op jit(solution)/shard_map/all_to_all | solution.py:19
  61.2 3.6 all-to-all-start.1
  65.6 33.9 %all-to-all-done.1 = bf16[8,64,1280]{2,1,0:T(8,128)(2,1)S(1)} async-done(((bf16[8,64,1280]{2,1,0:T(8,128)(2,1)}), bf16[8,64,1280]{2,1,0:T(8,128)(2,1)S(1)}, u32[]{:S(2)}, u32[]{:S(2)}) %all-to-all-start.1) | async-done | bytes 1310752 | tf_op jit(solution)/shard_map/all_to_all | solution.py:25
  100.4 2.0 copy.42
  102.3 1.9 reshape.248
  104.2 5.2 fusion.25
  109.6 4.0 gather_fusion
  114.9 7.6 %all-to-all-start.2 = ((bf16[32,32,448]{2,1,0:T(8,128)(2,1)}), bf16[32,32,448]{2,1,0:T(8,128)(2,1)S(1)}, u32[]{:S(2)}, u32[]{:S(2)}) async-start(bf16[32,32,448]{2,1,0:T(8,128)(2,1)} %select_select_fusion), calls=%async_computation.2 | async-start | bytes 2097152 | tf_op jit(solution)/shard_map/all_to_all | solution.py:121
  123.1 16.6 %all-to-all-done.2 = bf16[32,32,448]{2,1,0:T(8,128)(2,1)S(1)} async-done(((bf16[32,32,448]{2,1,0:T(8,128)(2,1)}), bf16[32,32,448]{2,1,0:T(8,128)(2,1)S(1)}, u32[]{:S(2)}, u32[]{:S(2)}) %all-to-all-start.2) | async-done | bytes 917536 | tf_op jit(solution)/shard_map/all_to_all | solution.py:121
  139.6 8.6 %stack.2 = bf16[32,112,3552]{2,1,0:T(8,128)(2,1)} broadcast(bf16[112,3552]{1,0:T(8,128)(2,1)S(1)} %concatenate.7), dimensions={1,2} | broadcast | bytes 26256384 | tf_op jit(solution)/shard_map/stack | solution.py:44
  148.2 5.3 all-to-all-start.3
  154.7 2.0 gather_fusion.1
  158.1 45.9 %all-gather.2.cloned.1.call-done = bf16[512,3584]{0,1:T(8,128)(2,1)} async-done(((bf16[512,448]{0,1:T(8,128)(2,1)}), bf16[512,3584]{0,1:T(8,128)(2,1)}) %all-gather.2.cloned.1.call-update) | async-done | bytes 3670032 | tf_op jit(solution)/shard_map/all_gather | solution.py:134
  204.0 2.9 fusion.7
  206.9 257.3 %all-to-all-done.3 = bf16[32,112,3552]{2,1,0:T(8,128)(2,1)} async-done(((bf16[32,112,3552]{2,1,0:T(8,128)(2,1)}), bf16[32,112,3552]{2,1,0:T(8,128)(2,1)}, u32[]{:S(2)}, u32[]{:S(2)}) %all-to-all-start.3) | async-done | bytes 25460768 | tf_op jit(solution)/shard_map/all_to_all | solution.py:44
  464.2 9.7 %fusion.5 = f32[512,1184]{0,1:T(8,128)S(1)} fusion(bf16[3584,3552]{1,0:T(8,128)(2,1)} %bitcast.22, bf16[512,3584]{0,1:T(8,128)(2,1)} %all-gather.2.cloned.1.call-done, f32[3584]{0:T(1024)S(1)} %copy-done.11, f32[512]{0:T(512)S(1)} %add_rsqrt_fusion.1), kind=kOutput, calls=%fused_computation.7 | convolution fusion | flops 4352638976 | bytes 15286272 | tf_op jit(solution)/shard_map/dot_general | solution.py:139
  473.9 24.9 %fusion.10 = bf16[512,3584]{1,0:T(8,128)(2,1)} fusion(bf16[3584,3552]{1,0:T(8,128)(2,1)} %bitcast.22, f32[512,1184]{0,1:T(8,128)S(1)} %fusion.5, bf16[512,3584]{0,1:T(8,128)(2,1)} %all-gather.2.cloned.1.call-done, f32[3584]{0:T(1024)S(1)} %copy-done.11, f32[512]{0:T(512)S(1)} %add_rsqrt_fusion.1), kind=kOutput, calls=%fused_computation.14 | convolution fusion | flops 8703410176 | bytes 28131328 | tf_op jit(solution)/shard_map/dot_general | solution.py:142
  498.8 1.6 constant_dynamic-slice_fusion
  500.7 57.7 %reduce-scatter.2.cloned.1.call-done = bf16[64,3584]{1,0:T(8,128)(2,1)} async-done(((bf16[512,3584]{1,0:T(8,128)(2,1)}), bf16[64,3584]{1,0:T(8,128)(2,1)}) %reduce-scatter.2.cloned.1.call-update) | async-done | bytes 458768 | tf_op jit(solution)/shard_map/reduce_scatter | solution.py:143
  558.4 1.9 add_convert_fusion
  (74 shorter events, 11.5 us)
Async XLA Ops:
  6.5 7.7 %copy-start = (bf16[160,1280]{1,0:T(8,128)(2,1)S(1)}, bf16[160,1280]{1,0:T(8,128)(2,1)}, u32[]{:S(2)}) copy-start(bf16[160,1280]{1,0:T(8,128)(2,1)} %param.18) | copy-start | bytes 1228804
  6.5 3.9 copy-start.2
  6.5 3.9 copy-start.10
  6.5 3.9 copy-start.12
  10.5 1.3 copy-start.8
  15.9 43.9 %all-to-all-start = ((bf16[8,64,1280]{2,1,0:T(8,128)(2,1)}), bf16[8,64,1280]{2,1,0:T(8,128)(2,1)S(1)}, u32[]{:S(2)}, u32[]{:S(2)}) async-start(bf16[8,64,1280]{2,1,0:T(8,128)(2,1)} %bitcast.15), calls=%async_computation | async-start | bytes 2621440 | tf_op jit(solution)/shard_map/all_to_all | solution.py:19
  60.0 4.8 copy-start.3
  60.0 5.0 copy-start.9
  60.0 5.0 copy-start.7
  61.2 38.3 %all-to-all-start.1 = ((bf16[8,64,1280]{2,1,0:T(8,128)(2,1)}), bf16[8,64,1280]{2,1,0:T(8,128)(2,1)S(1)}, u32[]{:S(2)}, u32[]{:S(2)}) async-start(bf16[8,64,1280]{2,1,0:T(8,128)(2,1)} %broadcast_in_dim.103), calls=%async_computation.1 | async-start | bytes 2621440 | tf_op jit(solution)/shard_map/all_to_all | solution.py:25
  113.6 8.9 %copy-start.4 = (bf16[112,1184]{1,0:T(8,128)(2,1)S(1)}, bf16[112,1184]{1,0:T(8,128)(2,1)}, u32[]{:S(2)}) copy-start(bf16[112,1184]{1,0:T(8,128)(2,1)} %param.25) | copy-start | bytes 795652
  113.6 8.9 %copy-start.5 = (bf16[112,1184]{1,0:T(8,128)(2,1)S(1)}, bf16[112,1184]{1,0:T(8,128)(2,1)}, u32[]{:S(2)}) copy-start(bf16[112,1184]{1,0:T(8,128)(2,1)} %param.26) | copy-start | bytes 795652
  113.6 8.9 %copy-start.6 = (bf16[1184,112]{0,1:T(8,128)(2,1)S(1)}, bf16[1184,112]{0,1:T(8,128)(2,1)}, u32[]{:S(2)}) copy-start(bf16[1184,112]{0,1:T(8,128)(2,1)} %param.27) | copy-start | bytes 795652
  114.9 24.8 %all-to-all-start.2 = ((bf16[32,32,448]{2,1,0:T(8,128)(2,1)}), bf16[32,32,448]{2,1,0:T(8,128)(2,1)S(1)}, u32[]{:S(2)}, u32[]{:S(2)}) async-start(bf16[32,32,448]{2,1,0:T(8,128)(2,1)} %select_select_fusion), calls=%async_computation.2 | async-start | bytes 2097152 | tf_op jit(solution)/shard_map/all_to_all | solution.py:121
  148.2 316.0 %all-to-all-start.3 = ((bf16[32,112,3552]{2,1,0:T(8,128)(2,1)}), bf16[32,112,3552]{2,1,0:T(8,128)(2,1)}, u32[]{:S(2)}, u32[]{:S(2)}) async-start(bf16[32,112,3552]{2,1,0:T(8,128)(2,1)} %stack.2), calls=%async_computation.3 | async-start | bytes 51380224 | tf_op jit(solution)/shard_map/all_to_all | solution.py:44
  153.6 50.4 %all-gather.2.cloned.1.call-start = ((), (), s32[]{:S(2)}) async-start(), calls=%async_computation.5 | async-start | bytes 4128768 | tf_op jit(solution)/shard_map/all_gather | solution.py:134
  156.9 307.3 %copy-start.11 = (f32[3584]{0:T(1024)S(1)}, f32[3584]{0:T(1024)}, u32[]{:S(2)}) copy-start(f32[3584]{0:T(1024)} %param.24) | copy-start | bytes 43012
  157.9 400.6 %reduce-scatter.2.cloned.1.call-start = ((), (), s32[]{:S(2)}) async-start(), calls=%async_computation.6 | async-start | bytes 4128768 | tf_op jit(solution)/shard_map/reduce_scatter | solution.py:143
  498.8 61.5 %copy-start.1 = (bf16[160,1280]{1,0:T(8,128)(2,1)S(1)}, bf16[160,1280]{1,0:T(8,128)(2,1)}, u32[]{:S(2)}) copy-start(bf16[160,1280]{1,0:T(8,128)(2,1)} %param.18) | copy-start | bytes 1228804
Sparse Core Ops, SparseCore 0:
  158.0 45.9 all-gather.1
  498.9 59.4 reduce-scatter.1
